TPU v7x, 128 devices: a whole 4x4x4 slice. The times are simulated.
128 devices in a mesh: pos: 16 (over x, y), obj: 8 (over z, core).
Axes of the slice: x: 4, y: 4, z: 4, core: 2. Of those that a mesh axis runs over, the one named last changes fastest.
Arguments:
- object_field: float32 [2, 4096, 6144], P(None, 'obj', 'pos'), may hold values from -5 to 5
- probe: float32 [2, 256, 256], replicated, may hold values from -5 to 5
- amplitude: bfloat16 [2048, 256, 256], P(('pos', 'obj')), may hold values from 0.19921875 to 3
- row_offset: int32 [2048], P(('pos', 'obj')), may hold values from 0 to 256
- col_offset: int32 [2048], P(('pos', 'obj')), may hold values from 0 to 128
- owner: int32 [2048], P(('pos', 'obj')), may hold values from 0 to 15, as said below
Outputs:
- new_object: float32 [2, 4096, 6144], P(None, 'obj', 'pos')
- new_probe: float32 [2, 256, 256], replicated
Inputs may be any that keep to these rules, and one draw needn't show every extreme that they name: Among the 16 positions of one device no owner is named more than 2 times; in each row band one owner is named exactly 2 times by every device.
All inputs are finite; a program needn't handle non-finite values.
Results may differ from a plain program's by a relative error of at most 0.005.
The roundings to bfloat16 on the way count: a program that leaves them out, or rounds other values in their place, can miss the bound.
Values may be sent and summed in bfloat16 or wider, within the bound.
A program may use at most 128 MiB of HBM per device.

v0:
```python
import math
import jax
import jax.numpy as jnp
from jax import lax
from jax.sharding import PartitionSpec as P


def padded_2(block, sides, width):
    for axis, dim in sides:
        count = lax.axis_size(axis)
        forward = [(i, i + 1) for i in range(count - 1)]
        forward.append((count - 1, 0))
        backward = [(target, source) for source, target in forward]
        low = lax.ppermute(
            lax.slice_in_dim(block, block.shape[dim] - width, None, axis=dim), axis, forward
        )
        high = lax.ppermute(lax.slice_in_dim(block, 0, width, axis=dim), axis, backward)
        block = jnp.concatenate([low, block, high], axis=dim)
    return block


def dft_tables(size):
    index = jnp.arange(size, dtype=jnp.int32)
    product = index[:, None] * index[None, :] % size
    angle = product.astype(jnp.float32) * (2.0 * math.pi / size)
    scale = 1.0 / math.sqrt(size)
    real_part = (jnp.cos(angle) * scale).astype(jnp.bfloat16)
    imag_part = (-jnp.sin(angle) * scale).astype(jnp.bfloat16)
    return (real_part, imag_part)


def left_apply(mat_re, mat_im, val_re, val_im):

    def product(matrix, values):
        return jnp.einsum("jk,bkl->bjl", matrix, values, preferred_element_type=jnp.float32)

    return (
        product(mat_re, val_re) - product(mat_im, val_im),
        product(mat_re, val_im) + product(mat_im, val_re),
    )


def right_apply(val_re, val_im, mat_re, mat_im):

    def product(values, matrix):
        return jnp.einsum("bjk,kl->bjl", values, matrix, preferred_element_type=jnp.float32)

    return (
        product(val_re, mat_re) - product(val_im, mat_im),
        product(val_re, mat_im) + product(val_im, mat_re),
    )


def position_terms(patches, amps, validity, probe, tables):
    four_re, four_im, conj_im = tables
    patch_re = patches[:, 0].astype(jnp.float32)
    patch_im = patches[:, 1].astype(jnp.float32)
    probe_re = probe[0]
    probe_im = probe[1]
    psi_re = (probe_re * patch_re - probe_im * patch_im).astype(jnp.bfloat16)
    psi_im = (probe_re * patch_im + probe_im * patch_re).astype(jnp.bfloat16)
    left_re, left_im = left_apply(four_re, four_im, psi_re, psi_im)
    wave_re, wave_im = right_apply(
        left_re.astype(jnp.bfloat16), left_im.astype(jnp.bfloat16), four_re, four_im
    )
    magnitude = jnp.sqrt(wave_re * wave_re + wave_im * wave_im)
    factor = 1.0 - amps.astype(jnp.float32) / jnp.maximum(magnitude, 0.5)
    diff_re = (wave_re * factor).astype(jnp.bfloat16)
    diff_im = (wave_im * factor).astype(jnp.bfloat16)
    back_re, back_im = left_apply(four_re, conj_im, diff_re, diff_im)
    chi_re, chi_im = right_apply(
        back_re.astype(jnp.bfloat16), back_im.astype(jnp.bfloat16), four_re, conj_im
    )
    chi_re = chi_re * validity[:, None, None]
    chi_im = chi_im * validity[:, None, None]
    grad_re = (probe_re * chi_re + probe_im * chi_im).astype(jnp.bfloat16)
    grad_im = (probe_re * chi_im - probe_im * chi_re).astype(jnp.bfloat16)
    term_re = jnp.sum(patch_re * chi_re + patch_im * chi_im, axis=0)
    term_im = jnp.sum(patch_re * chi_im - patch_im * chi_re, axis=0)
    return (jnp.stack([grad_re, grad_im], axis=1), jnp.stack([term_re, term_im]))


def run_terms(patches, amps, validity, probe, tables):
    count = patches.shape[0]
    size = patches.shape[2]
    batch_size = math.gcd(count, 8)
    groups = count // batch_size
    grouped = (
        patches.reshape(groups, batch_size, 2, size, size),
        amps.reshape(groups, batch_size, size, size),
        validity.reshape(groups, batch_size),
    )
    grads, terms = lax.map(
        lambda items: position_terms(items[0], items[1], items[2], probe, tables), grouped
    )
    return (grads.reshape(count, 2, size, size), jnp.sum(terms, axis=0))


def extract(tile, corners, size):
    zero = jnp.zeros((), jnp.int32)
    windows = jax.vmap(lambda row, col: lax.dynamic_slice(tile, (zero, row, col), (2, size, size)))(
        corners[:, 0], corners[:, 1]
    )
    return windows.astype(jnp.bfloat16)


def add_scaled(start_value, grads, corners, size):
    zero = jnp.zeros((), jnp.int32)

    def add_one(item, acc):
        corner = (zero, corners[item, 0], corners[item, 1])
        window = lax.dynamic_slice(acc, corner, (2, size, size))
        return lax.dynamic_update_slice(
            acc, window - 0.25 * grads[item].astype(jnp.float32), corner
        )

    return lax.fori_loop(0, grads.shape[0], add_one, start_value)


def shards(object_field, probe, amplitude, row_offset, col_offset, owner):
    n_pos = lax.axis_size("pos")
    n_obj = lax.axis_size("obj")
    pos_dev = amplitude.shape[0]
    size = amplitude.shape[1]
    capacity = max(2, pos_dev // n_pos + 1)
    slots = n_pos * capacity
    padded = padded_2(object_field.astype(jnp.bfloat16), (("pos", 2), ("obj", 1)), 1).astype(
        object_field.dtype
    )
    smooth = 4.0 * object_field - padded[:, :-2, 1:-1] - padded[:, 2:, 1:-1]
    smooth = smooth - padded[:, 1:-1, :-2] - padded[:, 1:-1, 2:]
    four_re, four_im = dft_tables(size)
    tables = (four_re, four_im, -four_im)
    onehot = (owner[:, None] == jnp.arange(n_pos, dtype=jnp.int32)[None, :]).astype(jnp.int32)
    earlier = jnp.cumsum(onehot, axis=0) - onehot
    ranking = jnp.sum(earlier * onehot, axis=1)
    target = owner * capacity + ranking
    matching = (target[:, None] == jnp.arange(slots, dtype=jnp.int32)[None, :]).astype(jnp.int32)
    source = jnp.sum(matching * jnp.arange(pos_dev, dtype=jnp.int32)[:, None], axis=0)
    filled = jnp.sum(matching, axis=0) > 0
    listing = jnp.stack([row_offset, col_offset, jnp.ones_like(row_offset)], axis=1)
    slot_info = jnp.where(filled[:, None], listing[source], 0).reshape(n_pos, capacity, 3)
    received = lax.all_to_all(slot_info, "pos", split_axis=0, concat_axis=0, tiled=True)
    items = received.shape[1]
    windows = extract(object_field, received.reshape(-1, 3), size)
    windows = windows.reshape(n_pos, items, 2, size, size)
    fetched = lax.all_to_all(windows, "pos", split_axis=0, concat_axis=0, tiled=True)
    mine = fetched.reshape(slots, 2, size, size)[target]
    grads, probe_part = run_terms(mine, amplitude, jnp.ones((pos_dev,), jnp.float32), probe, tables)
    grad_slots = jnp.where(filled[:, None, None, None], grads[source], jnp.zeros((), jnp.bfloat16))
    incoming = lax.all_to_all(
        grad_slots.reshape(n_pos, capacity, 2, size, size),
        "pos",
        split_axis=0,
        concat_axis=0,
        tiled=True,
    )
    incoming = incoming.reshape(slots, 2, size, size)
    corners = received.reshape(slots, 3)
    base = object_field - 0.125 * smooth
    new_object = add_scaled(base, incoming, corners, size)
    probe_grad = lax.psum(probe_part, ("pos", "obj"))
    n_total = pos_dev * n_pos * n_obj
    new_probe = probe - probe_grad * (1.0 / math.sqrt(n_total))
    return (new_object, new_probe)


def solution(mesh):
    placed = (
        P(None, "obj", "pos"),
        P(),
        P(("pos", "obj"), None, None),
        P(("pos", "obj")),
        P(("pos", "obj")),
        P(("pos", "obj")),
    )
    return jax.shard_map(
        shards, mesh=mesh, in_specs=placed, out_specs=(P(None, "obj", "pos"), P()), check_vma=False
    )
```

profile of v0, /device:TPU:15, one launch (start us, length us, event | category | flops | bytes accessed | tf_op | source)
XLA Modules:
  0.0 1008.5 jit_solution(17226852778361089383)
XLA Ops:
  12.1 6.8 all-to-all-start
  22.9 89.1 %while.29 = (s32[]{:T(128)}, bf16[2,512,384]{2,1,0:T(8,128)(2,1)S(1)}, s32[32,3]{0,1:T(4,128)S(1)}, bf16[32,2,256,256]{3,2,1,0:T(8,128)(2,1)}, s32[]{:T(128)}) while((s32[]{:T(128)}, bf16[2,512,384]{2,1,0:T(8,128)(2,1)S(1)}, s32[32,3]{0,1:T(4,128)S(1)}, bf16[32,2,256,256]{3,2,1,0:T(8,128)(2,1)}, s32[]{:T(128)}) %tuple.89), condition=%wide.while_cond, body=%wide.while_body.sunk | while | flops 2 | bytes 525929 | solution.py:101
  112.9 7.2 all-to-all-start.1
  120.1 130.6 %all-to-all-done.1 = bf16[16,2,2,256,256]{4,3,2,1,0:T(8,128)(2,1)} async-done(((bf16[16,2,2,256,256]{4,3,2,1,0:T(8,128)(2,1)}), bf16[16,2,2,256,256]{4,3,2,1,0:T(8,128)(2,1)}, u32[]{:S(2)}, u32[]{:S(2)}) %all-to-all-start.1) | async-done | bytes 8388640 | tf_op jit(solution)/shard_map/all_to_all | solution.py:147
  250.7 6.2 gather_fusion.1
  256.9 60.2 %while.30 = (s32[]{:T(128)}, bf16[2,8,2,256,256]{4,3,2,1,0:T(8,128)(2,1)}, f32[2,2,256,256]{3,2,1,0:T(8,128)S(1)}, f32[2,256,256]{2,1,0:T(8,128)S(1)}, bf16[2,8,...) while((s32[]{:T(128)}, ...), condition=%wide.region_7.8_spmd.clone.clone, body=%wide.region_4.7_spmd.clone.clone.sunk | while | flops 4348182528 | bytes 96470128 | solution.py:93
  282.5 3.0 fusion.253
  312.5 3.0 fusion.253
  317.1 7.5 gather_fusion.2
  324.6 7.2 broadcast_select_fusion
  331.8 9.4 all-to-all-start.2
  342.9 91.4 %collective-permute-done = bf16[2,512,1]{2,1,0:T(8,128)(2,1)S(1)} collective-permute-done((bf16[2,512,1]{2,1,0:T(8,128)(2,1)S(1)}, bf16[2,512,1]{2,1,0:T(8,128)(2,1)S(1)}, u32[]{:S(2)}, u32[]{:S(2)}) %collective-permute-start) | collective-permute-done | bytes 2080 | tf_op jit(solution)/shard_map/ppermute | solution.py:14
  435.7 11.3 %collective-permute-start.2 = (bf16[2,1,386]{2,1,0:T(2,128)(2,1)S(1)}, bf16[2,1,386]{2,1,0:T(2,128)(2,1)S(1)}, u32[]{:S(2)}, u32[]{:S(2)}) collective-permute-start(bf16[2,1,386]{2,1,0:T(2,128)(2,1)S(1)} %get-tuple-element.299), channel_id=1, source_target_pairs={{0,1},{1,2},{2,3},{3,4},{4,5},{5,6},{6,7},{7,0},{8,9},{9,10},{10,1... | collective-permute-start | bytes 4640 | tf_op jit(solution)/shard_map/ppermute | solution.py:14
  454.1 3.9 fusion.143
  458.0 151.4 %all-reduce.2.cloned.1.call-done = f32[2,256,256]{2,1,0:T(8,128)} async-done(((f32[2,256,256]{2,1,0:T(8,128)}), f32[2,256,256]{2,1,0:T(8,128)}) %all-reduce.2.cloned.1.call-update) | async-done | bytes 524304 | tf_op jit(solution)/shard_map/psum | solution.py:162
  611.3 390.4 %while.28 = (s32[]{:T(128)}, f32[2,512,384]{2,1,0:T(8,128)}, s32[32,3]{0,1:T(4,128)S(1)}, bf16[32,2,256,256]{3,2,1,0:T(8,128)(2,1)}, s32[]{:T(128)}, /*index=5*/s32[]{:T(128)}, s32[]{:T(128)}, s32[]{:T(128)}) while((s32[]{:T(128)}, f32[2,512,384]{2,1,0:T(8,128)}, s32[32,3]{0,1:T(4,128)S(1)}, bf16[32,2,256,256]{3,2,1,0:T(8,128)(2,1)}, ...), condition=%wide.region_9.10_spmd, body=%wide.region_8.9_spmd.sunk | while | flops 393224 | bytes 2359485 | solution.py:117
  617.2 6.4 dynamic_update_slice.24
  629.4 6.1 dynamic_update_slice.24
  641.4 6.5 dynamic_update_slice.24
  653.7 6.0 dynamic_update_slice.24
  665.7 6.5 dynamic_update_slice.24
  678.0 6.5 dynamic_update_slice.24
  690.4 6.5 dynamic_update_slice.24
  702.7 6.5 dynamic_update_slice.24
  715.1 6.5 dynamic_update_slice.24
  727.5 6.4 dynamic_update_slice.24
  739.8 6.5 dynamic_update_slice.24
  752.1 6.3 dynamic_update_slice.24
  764.3 6.3 dynamic_update_slice.24
  776.5 6.4 dynamic_update_slice.24
  788.7 6.4 dynamic_update_slice.24
  801.0 6.5 dynamic_update_slice.24
  813.4 6.0 dynamic_update_slice.24
  825.3 6.4 dynamic_update_slice.24
  837.5 6.5 dynamic_update_slice.24
  849.9 5.9 dynamic_update_slice.24
  861.7 6.2 dynamic_update_slice.24
  873.8 6.2 dynamic_update_slice.24
  885.8 6.4 dynamic_update_slice.24
  898.1 6.3 dynamic_update_slice.24
  910.3 6.5 dynamic_update_slice.24
  922.6 6.3 dynamic_update_slice.24
  934.8 6.1 dynamic_update_slice.24
  946.8 6.5 dynamic_update_slice.24
  959.1 6.0 dynamic_update_slice.24
  971.0 6.0 dynamic_update_slice.24
  982.9 6.5 dynamic_update_slice.24
  995.3 6.4 dynamic_update_slice.24
  (258 shorter events, 231.3 us)
Async XLA Ops:
  12.1 10.6 %all-to-all-start = ((s32[16,2,3]{2,1,0:T(2,128)}), s32[16,2,3]{2,1,0:T(2,128)S(1)}, u32[]{:S(2)}, u32[]{:S(2)}) async-start(s32[16,2,3]{2,1,0:T(2,128)} %copy.88), calls=%async_computation | async-start | bytes 32768 | tf_op jit(solution)/shard_map/all_to_all | solution.py:143
  22.8 89.2 %copy-start.6 = (s32[32,3]{0,1:T(4,128)}, s32[32,3]{0,1:T(4,128)S(1)}, u32[]{:S(2)}) copy-start(s32[32,3]{0,1:T(4,128)S(1)} %copy.109) | copy-start | bytes 1156
  112.0 0.9 copy-start
  112.9 137.8 %all-to-all-start.1 = ((bf16[16,2,2,256,256]{4,3,2,1,0:T(8,128)(2,1)}), bf16[16,2,2,256,256]{4,3,2,1,0:T(8,128)(2,1)}, u32[]{:S(2)}, u32[]{:S(2)}) async-start(bf16[16,2,2,256,256]{4,3,2,1,0:T(8,128)(2,1)} %bitcast.241), calls=%async_computation.1 | async-start | bytes 16777216 | tf_op jit(solution)/shard_map/all_to_all | solution.py:147
  250.7 6.2 copy-start.2
  268.2 1.6 copy-start.8
  298.3 1.6 copy-start.8
  317.1 7.5 copy-start.3
  331.8 9.4 copy-start.1
  331.8 279.5 %all-to-all-start.2 = ((bf16[16,2,2,256,256]{4,3,2,1,0:T(8,128)(2,1)}), bf16[16,2,2,256,256]{4,3,2,1,0:T(8,128)(2,1)}, u32[]{:S(2)}, u32[]{:S(2)}) async-start(bf16[16,2,2,256,256]{4,3,2,1,0:T(8,128)(2,1)} %broadcast_select_fusion), calls=%async_computation.2 | async-start | bytes 16777216 | tf_op jit(solution)/shard_map/all_to_all | solution.py:151
  341.2 268.2 %all-reduce.2.cloned.1.call-start = ((), (), s32[]{:S(2)}) async-start(), calls=%async_computation.3 | async-start | bytes 1048576 | tf_op jit(solution)/shard_map/psum | solution.py:162
  341.4 92.9 %collective-permute-start = (bf16[2,512,1]{2,1,0:T(8,128)(2,1)S(1)}, bf16[2,512,1]{2,1,0:T(8,128)(2,1)S(1)}, u32[]{:S(2)}, u32[]{:S(2)}) collective-permute-start(bf16[2,512,1]{2,1,0:T(8,128)(2,1)S(1)} %get-tuple-element.301), channel_id=1, source_target_pairs={{0,8},{8,16},{16,24},{24,32},{32,40},{40,48},{48,56},{56,64},{64,7... | collective-permute-start | bytes 6152 | tf_op jit(solution)/shard_map/ppermute | solution.py:14
  342.6 91.7 %collective-permute-start.1 = (bf16[2,512,1]{2,1,0:T(8,128)(2,1)S(1)}, bf16[2,512,1]{2,1,0:T(8,128)(2,1)S(1)}, u32[]{:S(2)}, u32[]{:S(2)}) collective-permute-start(bf16[2,512,1]{2,1,0:T(8,128)(2,1)S(1)} %get-tuple-element.302), channel_id=1, source_target_pairs={{8,0},{16,8},{24,16},{32,24},{40,32},{48,40},{56,48},{64,56},{72,6... | collective-permute-start | bytes 6152 | tf_op jit(solution)/shard_map/ppermute | solution.py:17
  434.3 0.7 copy-start.4
  435.0 0.7 copy-start.5
  435.7 12.1 %collective-permute-start.2 = (bf16[2,1,386]{2,1,0:T(2,128)(2,1)S(1)}, bf16[2,1,386]{2,1,0:T(2,128)(2,1)S(1)}, u32[]{:S(2)}, u32[]{:S(2)}) collective-permute-start(bf16[2,1,386]{2,1,0:T(2,128)(2,1)S(1)} %get-tuple-element.299), channel_id=1, source_target_pairs={{0,1},{1,2},{2,3},{3,4},{4,5},{5,6},{6,7},{7,0},{8,9},{9,10},{10,1... | collective-permute-start | bytes 4640 | tf_op jit(solution)/shard_map/ppermute | solution.py:14
  447.1 3.0 collective-permute-start.3
  454.1 157.2 %copy-start.7 = (s32[32,3]{0,1:T(4,128)S(1)}, s32[32,3]{0,1:T(4,128)}, u32[]{:S(2)}) copy-start(s32[32,3]{0,1:T(4,128)} %copy-done.6) | copy-start | bytes 1156
Sparse Core Ops, SparseCore 0:
  454.2 155.1 all-reduce.1
where the time goes:
time: 1020 us; the launch traced here: 1010 us
  waiting for transfers between devices  379 us (37%)
  local copies, waits for them, and re-layouts  335 us (33%)
  loops' own time  122 us (12%)
  other arithmetic  70.1 us (7%)
  matrix products  53 us (5%)
  starting transfers between devices  36.3 us (4%)
  between operations  14.1 us (1%)
    dynamic_update_slice x32, local copies, waits for them, and re-layouts, add_one(): lax.dynamic_update_slice(acc, window - 0.25 * grads[item].astype(jnp.floa...  203 us
    psum x1, waiting for transfers between devices, shards(): probe_grad = lax.psum(probe_part, ('pos', 'obj'))  151 us
    all_to_all x1, waiting for transfers between devices, shards(): lax.all_to_all(windows, 'pos', split_axis=0, concat_axis=0, tiled=True)  131 us
    another operation x1, loops' own time, add_scaled(): return lax.fori_loop(0, grads.shape[0], add_one, start_value)  121 us
    ppermute x2, waiting for transfers between devices, padded_2(): lax.ppermute(lax.slice_in_dim(block, block.shape[dim] - width, None, axis...  92.1 us
    gather x96, local copies, waits for them, and re-layouts  89.1 us
    sub x32, other arithmetic, add_one(): window - 0.25 * grads[item].astype(jnp.float32)  45.3 us
    dot_general x16, matrix products, product(): jnp.einsum('bjk,kl->bjl', values, matrix, preferred_element_type=jnp.floa...  28.6 us
  transfers between devices with their start and end apart: 8, of which 6 were waited for; matrix products, arithmetic and copies ran while one was open for 1% of the time, Pallas kernels for 0%

commit v1 on v0

--- a/solution.py
+++ b/solution.py
@@ -159,7 +159,7 @@
     corners = received.reshape(slots, 3)
     base = object_field - 0.125 * smooth
     new_object = add_scaled(base, incoming, corners, size)
-    probe_grad = lax.psum(probe_part, ("pos", "obj"))
+    probe_grad = lax.psum(lax.psum(probe_part, "pos"), "obj")
     n_total = pos_dev * n_pos * n_obj
     new_probe = probe - probe_grad * (1.0 / math.sqrt(n_total))
     return (new_object, new_probe)

time: 1020 us -> 970 us (0.951)
  waiting for transfers between devices: 379 us -> 339 us
    psum x1 -> x2, waiting for transfers between devices: 151 us -> 110 us  [shards(): probe_grad = lax.psum(lax.psum(probe_part, 'pos'), 'obj')]
  transfers between devices with their start and end apart: 8 -> 9, of which waited for: 6 -> 8; matrix products, arithmetic and copies ran while one was open for 1% -> 1% of each run, Pallas kernels for 0% -> 0%
where the time goes in v1:
time: 970 us; the launch traced here: 961 us
  waiting for transfers between devices  339 us (35%)
  local copies, waits for them, and re-layouts  334 us (34%)
  loops' own time  115 us (12%)
  other arithmetic  68.8 us (7%)
  matrix products  53 us (5%)
  starting transfers between devices  36.6 us (4%)
  between operations  14.1 us (1%)
    dynamic_update_slice x32, local copies, waits for them, and re-layouts, add_one(): lax.dynamic_update_slice(acc, window - 0.25 * grads[item].astype(jnp.floa...  203 us
    all_to_all x1, waiting for transfers between devices, shards(): lax.all_to_all(windows, 'pos', split_axis=0, concat_axis=0, tiled=True)  131 us
    another operation x1, loops' own time, add_scaled(): return lax.fori_loop(0, grads.shape[0], add_one, start_value)  114 us
    psum x2, waiting for transfers between devices, shards(): probe_grad = lax.psum(lax.psum(probe_part, 'pos'), 'obj')  110 us
    ppermute x2, waiting for transfers between devices, padded_2(): lax.ppermute(lax.slice_in_dim(block, block.shape[dim] - width, None, axis...  92.8 us
    gather x96, local copies, waits for them, and re-layouts  89.8 us
    sub x32, other arithmetic, add_one(): window - 0.25 * grads[item].astype(jnp.float32)  45.3 us
    dot_general x16, matrix products, product(): jnp.einsum('bjk,kl->bjl', values, matrix, preferred_element_type=jnp.floa...  28.6 us
  transfers between devices with their start and end apart: 9, of which 8 were waited for; matrix products, arithmetic and copies ran while one was open for 1% of the time, Pallas kernels for 0%

profile of v1, /device:TPU:15, one launch (start us, length us, event | category | flops | bytes accessed | tf_op | source)
XLA Modules:
  0.0 960.6 jit_solution(6573021338882997671)
XLA Ops:
  12.1 6.8 all-to-all-start
  22.9 89.9 %while.29 = (s32[]{:T(128)}, bf16[2,512,384]{2,1,0:T(8,128)(2,1)S(1)}, s32[32,3]{0,1:T(4,128)S(1)}, bf16[32,2,256,256]{3,2,1,0:T(8,128)(2,1)}, s32[]{:T(128)}) while((s32[]{:T(128)}, bf16[2,512,384]{2,1,0:T(8,128)(2,1)S(1)}, s32[32,3]{0,1:T(4,128)S(1)}, bf16[32,2,256,256]{3,2,1,0:T(8,128)(2,1)}, s32[]{:T(128)}) %tuple.89), condition=%wide.while_cond, body=%wide.while_body.sunk | while | flops 2 | bytes 525929 | solution.py:101
  113.6 7.2 all-to-all-start.1
  120.9 130.6 %all-to-all-done.1 = bf16[16,2,2,256,256]{4,3,2,1,0:T(8,128)(2,1)} async-done(((bf16[16,2,2,256,256]{4,3,2,1,0:T(8,128)(2,1)}), bf16[16,2,2,256,256]{4,3,2,1,0:T(8,128)(2,1)}, u32[]{:S(2)}, u32[]{:S(2)}) %all-to-all-start.1) | async-done | bytes 8388640 | tf_op jit(solution)/shard_map/all_to_all | solution.py:147
  251.5 6.2 gather_fusion.1
  257.7 60.2 %while.30 = (s32[]{:T(128)}, bf16[2,8,2,256,256]{4,3,2,1,0:T(8,128)(2,1)}, f32[2,2,256,256]{3,2,1,0:T(8,128)S(1)}, f32[2,256,256]{2,1,0:T(8,128)S(1)}, bf16[2,8,...) while((s32[]{:T(128)}, ...), condition=%wide.region_7.8_spmd.clone.clone, body=%wide.region_4.7_spmd.clone.clone.sunk | while | flops 4348182528 | bytes 96470128 | solution.py:93
  283.2 3.0 fusion.253
  317.9 7.1 gather_fusion.2
  325.0 7.2 broadcast_select_fusion
  332.2 9.2 all-to-all-start.2
  344.4 92.0 %collective-permute-done = bf16[2,512,1]{2,1,0:T(8,128)(2,1)S(1)} collective-permute-done((bf16[2,512,1]{2,1,0:T(8,128)(2,1)S(1)}, bf16[2,512,1]{2,1,0:T(8,128)(2,1)S(1)}, u32[]{:S(2)}, u32[]{:S(2)}) %collective-permute-start) | collective-permute-done | bytes 2080 | tf_op jit(solution)/shard_map/ppermute | solution.py:14
  437.8 11.7 %collective-permute-start.2 = (bf16[2,1,386]{2,1,0:T(2,128)(2,1)S(1)}, bf16[2,1,386]{2,1,0:T(2,128)(2,1)S(1)}, u32[]{:S(2)}, u32[]{:S(2)}) collective-permute-start(bf16[2,1,386]{2,1,0:T(2,128)(2,1)S(1)} %get-tuple-element.299), channel_id=1, source_target_pairs={{0,1},{1,2},{2,3},{3,4},{4,5},{5,6},{6,7},{7,0},{8,9},{9,10},{10,1... | collective-permute-start | bytes 4640 | tf_op jit(solution)/shard_map/ppermute | solution.py:14
  454.7 50.1 %all-reduce.3.cloned.1.call-done = f32[2,256,256]{2,1,0:T(8,128)} async-done(((f32[2,256,256]{2,1,0:T(8,128)}), f32[2,256,256]{2,1,0:T(8,128)}) %all-reduce.3.cloned.1.call-update) | async-done | bytes 524304 | tf_op jit(solution)/shard_map/psum | solution.py:162
  504.9 3.9 fusion.143
  508.8 60.3 %all-reduce.5.cloned.1.call-done = f32[2,256,256]{2,1,0:T(8,128)} async-done(((f32[2,256,256]{2,1,0:T(8,128)}), f32[2,256,256]{2,1,0:T(8,128)}) %all-reduce.5.cloned.1.call-update) | async-done | bytes 524304 | tf_op jit(solution)/shard_map/psum | solution.py:162
  571.0 382.8 %while.28 = (s32[]{:T(128)}, f32[2,512,384]{2,1,0:T(8,128)}, s32[32,3]{0,1:T(4,128)S(1)}, bf16[32,2,256,256]{3,2,1,0:T(8,128)(2,1)}, s32[]{:T(128)}, /*index=5*/s32[]{:T(128)}, s32[]{:T(128)}, s32[]{:T(128)}) while((s32[]{:T(128)}, f32[2,512,384]{2,1,0:T(8,128)}, s32[32,3]{0,1:T(4,128)S(1)}, bf16[32,2,256,256]{3,2,1,0:T(8,128)(2,1)}, ...), condition=%wide.region_9.10_spmd, body=%wide.region_8.9_spmd.sunk | while | flops 393224 | bytes 2359485 | solution.py:117
  576.6 6.4 dynamic_update_slice.24
  588.7 6.1 dynamic_update_slice.24
  600.4 6.5 dynamic_update_slice.24
  612.5 6.0 dynamic_update_slice.24
  624.2 6.5 dynamic_update_slice.24
  636.3 6.5 dynamic_update_slice.24
  648.4 6.5 dynamic_update_slice.24
  660.5 6.5 dynamic_update_slice.24
  672.7 6.5 dynamic_update_slice.24
  684.8 6.4 dynamic_update_slice.24
  696.9 6.5 dynamic_update_slice.24
  709.0 6.3 dynamic_update_slice.24
  720.9 6.3 dynamic_update_slice.24
  732.9 6.4 dynamic_update_slice.24
  744.9 6.4 dynamic_update_slice.24
  756.9 6.5 dynamic_update_slice.24
  769.0 6.0 dynamic_update_slice.24
  780.7 6.4 dynamic_update_slice.24
  792.7 6.5 dynamic_update_slice.24
  804.8 5.9 dynamic_update_slice.24
  816.4 6.2 dynamic_update_slice.24
  828.3 6.2 dynamic_update_slice.24
  840.1 6.4 dynamic_update_slice.24
  852.1 6.3 dynamic_update_slice.24
  864.0 6.5 dynamic_update_slice.24
  876.1 6.3 dynamic_update_slice.24
  888.1 6.1 dynamic_update_slice.24
  899.8 6.5 dynamic_update_slice.24
  911.9 6.0 dynamic_update_slice.24
  923.6 6.0 dynamic_update_slice.24
  935.3 6.5 dynamic_update_slice.24
  947.4 6.4 dynamic_update_slice.24
  (259 shorter events, 233.6 us)
Async XLA Ops:
  12.1 10.6 %all-to-all-start = ((s32[16,2,3]{2,1,0:T(2,128)}), s32[16,2,3]{2,1,0:T(2,128)S(1)}, u32[]{:S(2)}, u32[]{:S(2)}) async-start(s32[16,2,3]{2,1,0:T(2,128)} %copy.88), calls=%async_computation | async-start | bytes 32768 | tf_op jit(solution)/shard_map/all_to_all | solution.py:143
  22.8 90.0 %copy-start.5 = (s32[32,3]{0,1:T(4,128)}, s32[32,3]{0,1:T(4,128)S(1)}, u32[]{:S(2)}) copy-start(s32[32,3]{0,1:T(4,128)S(1)} %copy.109) | copy-start | bytes 1156
  112.8 0.9 copy-start
  113.6 137.8 %all-to-all-start.1 = ((bf16[16,2,2,256,256]{4,3,2,1,0:T(8,128)(2,1)}), bf16[16,2,2,256,256]{4,3,2,1,0:T(8,128)(2,1)}, u32[]{:S(2)}, u32[]{:S(2)}) async-start(bf16[16,2,2,256,256]{4,3,2,1,0:T(8,128)(2,1)} %bitcast.241), calls=%async_computation.1 | async-start | bytes 16777216 | tf_op jit(solution)/shard_map/all_to_all | solution.py:147
  251.5 6.2 copy-start.2
  268.9 1.6 copy-start.7
  299.0 1.6 copy-start.7
  332.2 238.8 %all-to-all-start.2 = ((bf16[16,2,2,256,256]{4,3,2,1,0:T(8,128)(2,1)}), bf16[16,2,2,256,256]{4,3,2,1,0:T(8,128)(2,1)}, u32[]{:S(2)}, u32[]{:S(2)}) async-start(bf16[16,2,2,256,256]{4,3,2,1,0:T(8,128)(2,1)} %broadcast_select_fusion), calls=%async_computation.2 | async-start | bytes 16777216 | tf_op jit(solution)/shard_map/all_to_all | solution.py:151
  341.5 1.3 copy-start.1
  341.5 163.4 %all-reduce.3.cloned.1.call-start = ((), (), s32[]{:S(2)}) async-start(), calls=%async_computation.3 | async-start | bytes 1048576 | tf_op jit(solution)/shard_map/psum | solution.py:162
  342.4 226.6 %all-reduce.5.cloned.1.call-start = ((), (), s32[]{:S(2)}) async-start(), calls=%async_computation.4 | async-start | bytes 1048576 | tf_op jit(solution)/shard_map/psum | solution.py:162
  342.9 93.6 %collective-permute-start = (bf16[2,512,1]{2,1,0:T(8,128)(2,1)S(1)}, bf16[2,512,1]{2,1,0:T(8,128)(2,1)S(1)}, u32[]{:S(2)}, u32[]{:S(2)}) collective-permute-start(bf16[2,512,1]{2,1,0:T(8,128)(2,1)S(1)} %get-tuple-element.301), channel_id=1, source_target_pairs={{0,8},{8,16},{16,24},{24,32},{32,40},{40,48},{48,56},{56,64},{64,7... | collective-permute-start | bytes 6152 | tf_op jit(solution)/shard_map/ppermute | solution.py:14
  344.1 92.4 %collective-permute-start.1 = (bf16[2,512,1]{2,1,0:T(8,128)(2,1)S(1)}, bf16[2,512,1]{2,1,0:T(8,128)(2,1)S(1)}, u32[]{:S(2)}, u32[]{:S(2)}) collective-permute-start(bf16[2,512,1]{2,1,0:T(8,128)(2,1)S(1)} %get-tuple-element.302), channel_id=1, source_target_pairs={{8,0},{16,8},{24,16},{32,24},{40,32},{48,40},{56,48},{64,56},{72,6... | collective-permute-start | bytes 6152 | tf_op jit(solution)/shard_map/ppermute | solution.py:17
  436.4 0.7 copy-start.3
  437.1 0.7 copy-start.4
  437.8 12.5 %collective-permute-start.2 = (bf16[2,1,386]{2,1,0:T(2,128)(2,1)S(1)}, bf16[2,1,386]{2,1,0:T(2,128)(2,1)S(1)}, u32[]{:S(2)}, u32[]{:S(2)}) collective-permute-start(bf16[2,1,386]{2,1,0:T(2,128)(2,1)S(1)} %get-tuple-element.299), channel_id=1, source_target_pairs={{0,1},{1,2},{2,3},{3,4},{4,5},{5,6},{6,7},{7,0},{8,9},{9,10},{10,1... | collective-permute-start | bytes 4640 | tf_op jit(solution)/shard_map/ppermute | solution.py:14
  449.6 3.3 collective-permute-start.3
  504.9 66.1 %copy-start.6 = (s32[32,3]{0,1:T(4,128)S(1)}, s32[32,3]{0,1:T(4,128)}, u32[]{:S(2)}) copy-start(s32[32,3]{0,1:T(4,128)} %copy-done.5) | copy-start | bytes 1156
Sparse Core Ops, SparseCore 0:
  346.1 158.7 all-reduce.2
  507.3 61.7 all-reduce.4
